TPU v7x, 32 devices: a whole 2x2x4 slice. The times are simulated.
32 devices in a mesh: phys: 4 (over y, x), row: 2 (over core), col: 4 (over z).
Axes of the slice: x: 2, y: 2, z: 4, core: 2. Of those that a mesh axis runs over, the one named last changes fastest.
Arguments:
- rho_sites: bfloat16 [1, 16, 2048, 2048], P(None, 'phys', 'row', 'col'), may hold values from -0.0625 to 0.0625
- sigma_sites: bfloat16 [1, 16, 2048, 2048], P(None, 'phys', 'row', 'col'), may hold values from -0.0625 to 0.0625
- environment: float32 [2048, 2048], P('row', 'col'), may hold values from -6 to 6
Outputs:
- new_environment: float32 [2048, 2048], P('row', 'col')
All inputs are finite; a program needn't handle non-finite values.
Results may differ from a plain program's by a relative error of at most 0.004.
Values may be sent and summed in bfloat16 or wider, within the bound.
A program may use at most 128 MiB of HBM per device.

v0:
```python
import jax
import jax.numpy as jnp
from jax import lax
from jax.sharding import PartitionSpec as P


def per_device(rho_sites, sigma_sites, environment):
    env = environment
    rho_block = rho_sites[0]
    sigma_block = sigma_sites[0]
    env_b = env.astype(jnp.bfloat16)
    env_whole = lax.all_gather(env_b, "col", axis=1, tiled=True)
    half = jnp.einsum(
        "ik,pkl->pil",
        env_whole,
        lax.all_gather(sigma_block, "row", axis=1, tiled=True),
        preferred_element_type=jnp.float32,
    ).astype(jnp.bfloat16)
    partial_env = jnp.einsum(
        "pij,pil->jl",
        lax.all_gather(rho_block, "col", axis=2, tiled=True),
        half,
        preferred_element_type=jnp.float32,
    )
    row_part = lax.psum_scatter(partial_env, "row", scatter_dimension=0, tiled=True)
    env = lax.psum(row_part, "phys")
    return env


def solution(mesh):
    placed = (P(None, "phys", "row", "col"), P(None, "phys", "row", "col"), P("row", "col"))
    return jax.shard_map(
        per_device, mesh=mesh, in_specs=placed, out_specs=P("row", "col"), check_vma=False
    )
```

profile of v0, /device:TPU:0, one launch (start us, length us, event | category | flops | bytes accessed | tf_op | source)
XLA Modules:
  0.0 524.7 jit_solution(5357533425166158105)
XLA Ops:
  6.5 0.0 all-gather.6.cloned.1.call-start
  6.5 2.7 convert_element_type.9
  9.2 0.0 all-gather.6.cloned.1.call-update
  9.3 0.0 all-gather.8.cloned.1.call-start
  9.3 0.7 all-gather.8.cloned.1.call-update
  10.0 0.0 all-gather.10.cloned.1.call-start
  10.1 0.7 all-gather.10.cloned.1.call-update
  10.7 0.0 reduce-scatter.2.cloned.1.call-start
  10.8 82.1 %all-gather.6.cloned.1.call-done = bf16[1024,2048]{1,0:T(8,128)(2,1)} async-done(((bf16[1024,512]{1,0:T(8,128)(2,1)}), bf16[1024,2048]{1,0:T(8,128)(2,1)}) %all-gather.6.cloned.1.call-update) | async-done | bytes 4194320 | tf_op jit(solution)/shard_map/all_gather | solution.py:12
  92.9 19.9 %all-gather.8.cloned.1.call-done = bf16[1,4,2048,512]{3,2,1,0:T(8,128)(2,1)} async-done(((bf16[1,4,1024,512]{3,2,1,0:T(8,128)(2,1)}), bf16[1,4,2048,512]{3,2,1,0:T(8,128)(2,1)}) %all-gather.8.cloned.1.call-update) | async-done | bytes 8388624 | tf_op jit(solution)/shard_map/all_gather | solution.py:16
  112.8 289.5 %all-gather.10.cloned.1.call-done = bf16[1,4,1024,2048]{3,2,1,0:T(8,128)(2,1)} async-done(((bf16[1,4,1024,512]{3,2,1,0:T(8,128)(2,1)}), bf16[1,4,1024,2048]{3,2,1,0:T(8,128)(2,1)}) %all-gather.10.cloned.1.call-update) | async-done | bytes 16777232 | tf_op jit(solution)/shard_map/all_gather | solution.py:21
  402.3 29.0 %fusion.15 = f32[2048,512]{0,1:T(8,128)} fusion(bf16[1,4,1024,2048]{3,2,1,0:T(8,128)(2,1)} %all-gather.10.cloned.1.call-done, bf16[1024,2048]{1,0:T(8,128)(2,1)} %all-gather.6.cloned.1.call-done, bf16[1,4,2048,512]{3,2,1,0:T(8,128)(2,1)} %all-gather.8.cloned.1.call-done), kind=kOutput, calls=%fused_computation.7 | convolution fusion | flops 17181966336 | bytes 33554432 | tf_op jit(solution)/shard_map/pij,pil->jl/dot_general | solution.py:19
  431.3 0.0 reduce-scatter.2.cloned.1.call-update
  431.3 0.0 all-reduce.2.cloned.1.call-start
  431.4 10.2 %reduce-scatter.2.cloned.1.call-done = f32[1024,512]{0,1:T(8,128)} async-done(((f32[2048,512]{0,1:T(8,128)}), f32[1024,512]{0,1:T(8,128)}) %reduce-scatter.2.cloned.1.call-update) | async-done | bytes 2097168 | tf_op jit(solution)/shard_map/reduce_scatter | solution.py:25
  441.6 0.0 all-reduce.2.cloned.1.call-update
  441.6 73.7 %all-reduce.2.cloned.1.call-done = f32[1024,512]{0,1:T(8,128)} async-done(((f32[1024,512]{0,1:T(8,128)}), f32[1024,512]{0,1:T(8,128)}) %all-reduce.2.cloned.1.call-update) | async-done | bytes 2097168 | tf_op jit(solution)/shard_map/psum | solution.py:26
  515.3 2.9 copy.4
Async XLA Ops:
  6.5 86.3 %all-gather.6.cloned.1.call-start = ((), (), s32[]{:S(2)}) async-start(), calls=%async_computation.1 | async-start | bytes 5242880 | tf_op jit(solution)/shard_map/all_gather | solution.py:12
  9.3 103.5 %all-gather.8.cloned.1.call-start = ((), (), s32[]{:S(2)}) async-start(), calls=%async_computation.4 | async-start | bytes 12582912 | tf_op jit(solution)/shard_map/all_gather | solution.py:16
  10.0 392.3 %all-gather.10.cloned.1.call-start = ((), (), s32[]{:S(2)}) async-start(), calls=%async_computation.5 | async-start | bytes 20971520 | tf_op jit(solution)/shard_map/all_gather | solution.py:21
  10.7 430.8 %reduce-scatter.2.cloned.1.call-start = ((), (), s32[]{:S(2)}) async-start(), calls=%async_computation.2 | async-start | bytes 6291456 | tf_op jit(solution)/shard_map/reduce_scatter | solution.py:25
  431.3 84.0 %all-reduce.2.cloned.1.call-start = ((), (), s32[]{:S(2)}) async-start(), calls=%async_computation.3 | async-start | bytes 4194304 | tf_op jit(solution)/shard_map/psum | solution.py:26
Sparse Core Ops, SparseCore 0:
  9.4 83.4 all-gather.5
  94.4 18.3 all-gather.7
  114.4 287.9 all-gather.9
  431.5 10.0 reduce-scatter.1
  444.5 70.7 all-reduce.1
where the time goes:
time: 525 us
  waiting for transfers between devices  477 us (91%)
  matrix products  29 us (6%)
  between operations  13.1 us (2%)
    all_gather x1, waiting for transfers between devices, per_device(): lax.all_gather(rho_block, 'col', axis=2, tiled=True)  290 us
    all_gather x1, waiting for transfers between devices, per_device(): env_whole = lax.all_gather(env_b, 'col', axis=1, tiled=True)  82.1 us
    psum x1, waiting for transfers between devices, per_device(): env = lax.psum(row_part, 'phys')  73.7 us
    dot_general x1, matrix products, per_device(): jnp.einsum('pij,pil->jl', lax.all_gather(rho_block, 'col', axis=2, tiled=...  29 us
    all_gather x1, waiting for transfers between devices, per_device(): lax.all_gather(sigma_block, 'row', axis=1, tiled=True)  19.9 us
  transfers between devices with their start and end apart: 5, of which 5 were waited for; matrix products, arithmetic and copies ran while one was open for 0% of the time, Pallas kernels for 0%

commit v1 on v0

--- a/solution.py
+++ b/solution.py
@@ -23,7 +23,19 @@
         preferred_element_type=jnp.float32,
     )
     row_part = lax.psum_scatter(partial_env, "row", scatter_dimension=0, tiled=True)
-    env = lax.psum(row_part, "phys")
+
+    def shapes_unite(xin):
+        degree = lax.axis_size("phys")
+        work_now, h_now = (xin, 0)
+        while 1 << h_now < degree:
+            g_now = lax.ppermute(
+                work_now, axis_name="phys", perm=[(nth, nth ^ 1 << h_now) for nth in range(degree)]
+            )
+            work_now = work_now + g_now
+            h_now = h_now + 1
+        return work_now
+
+    env = shapes_unite(row_part)
     return env
 
 

time: 525 us -> 548 us (1.044)
  waiting for transfers between devices: 477 us -> 495 us
    ppermute x0 -> x2, waiting for transfers between devices: none -> 91.5 us  [shapes_unite(): lax.ppermute(work_now, axis_name='phys', perm=[(nth, nth ^ 1 << h_now) fo...]
    psum x1 -> x0, waiting for transfers between devices: 73.7 us -> none  [per_device(): env = lax.psum(row_part, 'phys')]
  transfers between devices with their start and end apart: 5 -> 6, of which waited for: 5 -> 6; matrix products, arithmetic and copies ran while one was open for 0% -> 0% of each run, Pallas kernels for 0% -> 0%
where the time goes in v1:
time: 548 us
  waiting for transfers between devices  495 us (90%)
  matrix products  29.2 us (5%)
  between operations  13.1 us (2%)
    all_gather x1, waiting for transfers between devices, per_device(): lax.all_gather(rho_block, 'col', axis=2, tiled=True)  290 us
    ppermute x2, waiting for transfers between devices, shapes_unite(): lax.ppermute(work_now, axis_name='phys', perm=[(nth, nth ^ 1 << h_now) fo...  91.5 us
    all_gather x1, waiting for transfers between devices, per_device(): env_whole = lax.all_gather(env_b, 'col', axis=1, tiled=True)  82.1 us
    dot_general x1, matrix products, per_device(): jnp.einsum('pij,pil->jl', lax.all_gather(rho_block, 'col', axis=2, tiled=...  29.2 us
    all_gather x1, waiting for transfers between devices, per_device(): lax.all_gather(sigma_block, 'row', axis=1, tiled=True)  19.9 us
  transfers between devices with their start and end apart: 6, of which 6 were waited for; matrix products, arithmetic and copies ran while one was open for 0% of the time, Pallas kernels for 0%

profile of v1, /device:TPU:0, one launch (start us, length us, event | category | flops | bytes accessed | tf_op | source)
XLA Modules:
  0.0 547.6 jit_solution(5187695963952920396)
XLA Ops:
  6.5 0.0 all-gather.6.cloned.1.call-start
  6.5 2.7 convert_element_type.9
  9.2 0.0 all-gather.6.cloned.1.call-update
  9.3 0.0 all-gather.8.cloned.1.call-start
  9.3 0.7 all-gather.8.cloned.1.call-update
  10.0 0.0 all-gather.10.cloned.1.call-start
  10.1 0.7 all-gather.10.cloned.1.call-update
  10.7 0.0 reduce-scatter.2.cloned.1.call-start
  10.8 82.1 %all-gather.6.cloned.1.call-done = bf16[1024,2048]{1,0:T(8,128)(2,1)} async-done(((bf16[1024,512]{1,0:T(8,128)(2,1)}), bf16[1024,2048]{1,0:T(8,128)(2,1)}) %all-gather.6.cloned.1.call-update) | async-done | bytes 4194320 | tf_op jit(solution)/shard_map/all_gather | solution.py:12
  92.9 19.9 %all-gather.8.cloned.1.call-done = bf16[1,4,2048,512]{3,2,1,0:T(8,128)(2,1)} async-done(((bf16[1,4,1024,512]{3,2,1,0:T(8,128)(2,1)}), bf16[1,4,2048,512]{3,2,1,0:T(8,128)(2,1)}) %all-gather.8.cloned.1.call-update) | async-done | bytes 8388624 | tf_op jit(solution)/shard_map/all_gather | solution.py:16
  112.8 289.5 %all-gather.10.cloned.1.call-done = bf16[1,4,1024,2048]{3,2,1,0:T(8,128)(2,1)} async-done(((bf16[1,4,1024,512]{3,2,1,0:T(8,128)(2,1)}), bf16[1,4,1024,2048]{3,2,1,0:T(8,128)(2,1)}) %all-gather.10.cloned.1.call-update) | async-done | bytes 16777232 | tf_op jit(solution)/shard_map/all_gather | solution.py:21
  402.3 29.2 %fusion.15 = f32[2048,512]{0,1:T(8,128)} fusion(bf16[1,4,1024,2048]{3,2,1,0:T(8,128)(2,1)} %all-gather.10.cloned.1.call-done, bf16[1024,2048]{1,0:T(8,128)(2,1)} %all-gather.6.cloned.1.call-done, bf16[1,4,2048,512]{3,2,1,0:T(8,128)(2,1)} %all-gather.8.cloned.1.call-done), kind=kOutput, calls=%fused_computation.7 | convolution fusion | flops 17181966336 | bytes 33554432 | tf_op jit(solution)/shard_map/pij,pil->jl/dot_general | solution.py:19
  431.5 0.0 reduce-scatter.2.cloned.1.call-update
  431.5 10.2 %reduce-scatter.2.cloned.1.call-done = f32[1024,512]{0,1:T(8,128)} async-done(((f32[2048,512]{0,1:T(8,128)}), f32[1024,512]{0,1:T(8,128)}) %reduce-scatter.2.cloned.1.call-update) | async-done | bytes 2097168 | tf_op jit(solution)/shard_map/reduce_scatter | solution.py:25
  441.8 1.8 collective-permute-start
  443.6 46.2 %collective-permute-done = f32[1024,512]{0,1:T(8,128)S(1)} collective-permute-done((f32[1024,512]{0,1:T(8,128)}, f32[1024,512]{0,1:T(8,128)S(1)}, u32[]{:S(2)}, u32[]{:S(2)}) %collective-permute-start) | collective-permute-done | bytes 2097184 | tf_op jit(solution)/shard_map/ppermute | solution.py:31
  489.8 2.0 add.8
  491.8 1.8 collective-permute-start.1
  493.6 45.3 %collective-permute-done.1 = f32[1024,512]{0,1:T(8,128)S(1)} collective-permute-done((f32[1024,512]{0,1:T(8,128)S(1)}, f32[1024,512]{0,1:T(8,128)S(1)}, u32[]{:S(2)}, u32[]{:S(2)}) %collective-permute-start.1) | collective-permute-done | bytes 2097184 | tf_op jit(solution)/shard_map/ppermute | solution.py:31
  538.9 0.4 add.9
  539.2 1.8 copy.4
Async XLA Ops:
  6.5 86.3 %all-gather.6.cloned.1.call-start = ((), (), s32[]{:S(2)}) async-start(), calls=%async_computation.1 | async-start | bytes 5242880 | tf_op jit(solution)/shard_map/all_gather | solution.py:12
  9.3 103.5 %all-gather.8.cloned.1.call-start = ((), (), s32[]{:S(2)}) async-start(), calls=%async_computation.3 | async-start | bytes 12582912 | tf_op jit(solution)/shard_map/all_gather | solution.py:16
  10.0 392.3 %all-gather.10.cloned.1.call-start = ((), (), s32[]{:S(2)}) async-start(), calls=%async_computation.4 | async-start | bytes 20971520 | tf_op jit(solution)/shard_map/all_gather | solution.py:21
  10.7 431.0 %reduce-scatter.2.cloned.1.call-start = ((), (), s32[]{:S(2)}) async-start(), calls=%async_computation.2 | async-start | bytes 6291456 | tf_op jit(solution)/shard_map/reduce_scatter | solution.py:25
  441.8 48.1 %collective-permute-start = (f32[1024,512]{0,1:T(8,128)}, f32[1024,512]{0,1:T(8,128)S(1)}, u32[]{:S(2)}, u32[]{:S(2)}) collective-permute-start(f32[1024,512]{0,1:T(8,128)} %reduce-scatter.2.cloned.1.call-done), channel_id=1, source_target_pairs={{0,8},{8,0},{16,24},{24,16},{1,9},{9,1},{17,25},{25,17},{2,10},{10... | collective-permute-start | bytes 6291464 | tf_op jit(solution)/shard_map/ppermute | solution.py:31
  491.8 47.1 %collective-permute-start.1 = (f32[1024,512]{0,1:T(8,128)S(1)}, f32[1024,512]{0,1:T(8,128)S(1)}, u32[]{:S(2)}, u32[]{:S(2)}) collective-permute-start(f32[1024,512]{0,1:T(8,128)S(1)} %add.8), channel_id=1, source_target_pairs={{0,16},{8,24},{16,0},{24,8},{1,17},{9,25},{17,1},{25,9},{2,18},{10... | collective-permute-start | bytes 6291464 | tf_op jit(solution)/shard_map/ppermute | solution.py:31
Sparse Core Ops, SparseCore 0:
  9.4 83.4 all-gather.5
  94.4 18.3 all-gather.7
  114.4 287.9 all-gather.9
  431.6 10.0 reduce-scatter.1
